TPU v7x, 32 devices: a whole 2x2x4 slice. The times are simulated.
32 devices in a mesh: parts: 2 (over y), seq: 8 (over z, core), rep: 2 (over x), head: 1.
Axes of the slice: x: 2, y: 2, z: 4, core: 2. Of those that a mesh axis runs over, the one named last changes fastest.
Arguments:
- activations: bfloat16 [4, 1024, 2048], P(('parts', 'rep'), 'seq', 'head'), parts along dimension 0, may hold values from -6 to 6
- value_weight: bfloat16 [2048, 2048], P(('seq', 'rep'), 'head'), may hold values from -0.125 to 0.125
- query_in: bfloat16 [4, 1024, 2048], P(('parts', 'rep'), 'seq', 'head'), parts along dimension 0, may hold values from -6 to 6
- key_in: bfloat16 [4, 1024, 2048], P(('parts', 'rep'), 'seq', 'head'), parts along dimension 0, may hold values from -6 to 6
- grad_out: bfloat16 [4, 1024, 2048], P(('parts', 'rep'), 'seq', 'head'), parts along dimension 0, may hold values from -6 to 6
- conv_kernel: float32 [3, 4, 2048], P(None, None, 'head'), may hold values from -3 to 3
- log_gate: float32 [4, 16, 1024], P(('parts', 'rep'), 'head', 'seq'), parts along dimension 0, as said below
Outputs:
- attn_out: bfloat16 [4, 1024, 2048], P(('parts', 'rep'), 'seq', 'head'), parts along dimension 0
- grad_query: bfloat16 [4, 1024, 2048], P(('parts', 'rep'), 'seq', 'head'), parts along dimension 0
- grad_key: bfloat16 [4, 1024, 2048], P(('parts', 'rep'), 'seq', 'head'), parts along dimension 0
- grad_x: bfloat16 [4, 1024, 2048], P(('parts', 'rep'), 'seq', 'head'), parts along dimension 0
- grad_w: float32 [4096, 2048], P(('parts', 'seq', 'rep'), 'head'), parts along dimension 0
- grad_conv: float32 [6, 4, 2048], P('parts', None, 'head'), parts along dimension 0
There are 2 independent parts, one for each index of `parts`. A program takes and returns all parts, laid end to end along the dimension named above; an argument that names none is the same for every part. Nothing has to cross between parts.
Inputs may be any that keep to these rules, and one draw needn't show every extreme that they name: `log_gate`: every entry is below zero.
All inputs are finite; a program needn't handle non-finite values.
Results may differ from a plain program's by a relative error of at most 0.015.
Values may be sent and summed in bfloat16 or wider, within the bound.
A program may use at most 128 MiB of HBM per device.

v0:
```python
import math
import jax
import jax.numpy as jnp
from jax import lax
from jax.sharding import PartitionSpec as P

EPSILON = 1e-06


def shifted(block, axis, distance):
    devices = range(lax.axis_size(axis))
    route = [(i - distance, i) for i in devices if i - distance in devices]
    return lax.ppermute(block, axis, route)


def prefix(part, axis, combine, identity, reverse):
    count = lax.axis_size(axis)
    place = lax.axis_index(axis)
    ahead = count - 1 - place if reverse else place
    gathered = jax.tree.map(lambda a: lax.all_gather(a, axis), part)
    state = jax.tree.map(lambda a, e: jnp.zeros_like(a) + jnp.asarray(e, a.dtype), part, identity)

    def one(step, state):
        source = count - 1 - step if reverse else step
        return combine(
            state, jax.tree.map(lambda a: lax.dynamic_index_in_dim(a, source, 0, False), gathered)
        )

    return lax.fori_loop(0, ahead, one, state)


def carried_in(value, axis, combine, identity, reverse):
    length, mine = (lax.axis_size(axis), lax.axis_index(axis))
    everything = jax.tree.map(
        lambda part, kind: lax.all_gather(part.astype(kind), axis),
        value,
        (jnp.bfloat16, jnp.bfloat16),
    )
    start = jax.tree.map(
        lambda part, zero: jnp.broadcast_to(jnp.asarray(zero, part.dtype), part.shape),
        value,
        identity,
    )

    def step(k, before):
        at = length - 1 - k if reverse else k
        reached = at > mine if reverse else at < mine
        new = combine(
            before, jax.tree.map(lambda part, own: part[at].astype(own.dtype), everything, value)
        )
        return jax.tree.map(lambda a, b: jnp.where(reached, a, b), new, before)

    return lax.fori_loop(0, length, step, start)


def scanned(decay, state, axis, reverse):
    count = lax.axis_size(axis)
    direction = -1 if reverse else 1
    distance = 1
    while distance < count:
        far_decay, far_state = shifted((decay, state), axis, direction * distance)
        decay, state = chain_join((far_decay, far_state), (decay, state))
        distance *= 2
    return shifted(state, axis, direction)


def chain_join(earlier, following):
    return (earlier[0] * following[0], following[0][:, None, None] * earlier[1] + following[1])


def causal_filter(stream_rows, previous, kernel_taps):
    rim_rows = previous.shape[0]
    length = stream_rows.shape[0]
    extended = jnp.concatenate([previous, stream_rows], axis=0).astype(jnp.float32)
    result = jnp.zeros(stream_rows.shape, jnp.float32)
    for offset in range(kernel_taps.shape[0]):
        result = (
            result + kernel_taps[offset] * extended[rim_rows - offset : rim_rows - offset + length]
        )
    return result


def filter_back(post_rows, following_rows, kernel_taps):
    length = post_rows.shape[0]
    extended = jnp.concatenate([post_rows, following_rows], axis=0)
    result = jnp.zeros(post_rows.shape, jnp.float32)
    for offset in range(kernel_taps.shape[0]):
        result = result + kernel_taps[offset] * extended[offset : offset + length]
    return result


def tap_sums(post_rows, stream_rows, previous, kernel_width):
    rim_rows = previous.shape[0]
    length = stream_rows.shape[0]
    extended = jnp.concatenate([previous, stream_rows], axis=0).astype(jnp.float32)
    return jnp.stack(
        [
            jnp.sum(post_rows * extended[rim_rows - offset : rim_rows - offset + length], axis=0)
            for offset in range(kernel_width)
        ]
    )


def local(activations, value_weight, query_in, key_in, grad_out, conv_kernel, log_gate):
    tok_rows = query_in.shape[1]
    channels = query_in.shape[2]
    head_count = log_gate.shape[1]
    head_size = channels // head_count
    kernel_width = conv_kernel.shape[1]
    rim_rows = kernel_width - 1
    grad_scale = 1.0 / math.sqrt(lax.axis_size("seq") * lax.axis_size("rep") * tok_rows)
    query_rows = query_in[0]
    key_rows = key_in[0]
    gathered = lax.all_gather(activations, "head", axis=2, tiled=True)[0]
    columns = gathered
    value_f32 = jnp.dot(
        columns,
        lax.all_gather(value_weight, ("seq", "rep"), axis=0, tiled=True),
        preferred_element_type=jnp.float32,
    )
    value_raw = value_f32.astype(jnp.bfloat16)
    before_all = shifted(
        jnp.stack(
            [
                query_rows[tok_rows - rim_rows :],
                key_rows[tok_rows - rim_rows :],
                value_raw[tok_rows - rim_rows :],
            ]
        ),
        "seq",
        1,
    )
    before = (before_all[0], before_all[1], before_all[2])
    raw_rows = (query_rows, key_rows, value_raw)
    convolved = [
        causal_filter(raw_rows[which], before[which], conv_kernel[which]).astype(jnp.bfloat16)
        for which in range(3)
    ]
    query_heads = convolved[0].reshape(tok_rows, head_count, head_size)
    key_heads = convolved[1].reshape(tok_rows, head_count, head_size)
    value_heads = convolved[2].reshape(tok_rows, head_count, head_size)
    cumulative = jnp.cumsum(log_gate[0], axis=1)
    final_cum = cumulative[:, -1]
    block_decay = jnp.exp(final_cum)
    rising = jnp.exp(cumulative).T[:, :, None]
    shrink = jnp.exp(final_cum[:, None] - cumulative).T[:, :, None]
    mixing = jnp.exp(-jnp.abs(cumulative[:, :, None] - cumulative[:, None, :]))
    scores = (
        mixing
        * jnp.einsum("thd,shd->hts", query_heads, key_heads, preferred_element_type=jnp.float32)
    ).astype(jnp.bfloat16)
    fwd_sum = jnp.einsum(
        "thd,the->hde",
        (shrink * key_heads).astype(jnp.bfloat16),
        value_heads,
        preferred_element_type=jnp.float32,
    )
    back_sum = jnp.einsum(
        "thd,the->hde",
        (rising * key_heads).astype(jnp.bfloat16),
        value_heads,
        preferred_element_type=jnp.float32,
    )
    identity = (
        jnp.ones((head_count,), jnp.float32),
        jnp.zeros((head_count, head_size, head_size), jnp.float32),
    )
    left_b = scanned(block_decay, fwd_sum, "seq", False).astype(jnp.bfloat16)
    right_b = scanned(block_decay, back_sum, "seq", True).astype(jnp.bfloat16)
    attn = rising * jnp.einsum(
        "thd,hde->the", query_heads, left_b, preferred_element_type=jnp.float32
    )
    attn = attn + shrink * jnp.einsum(
        "thd,hde->the", query_heads, right_b, preferred_element_type=jnp.float32
    )
    attn = attn + jnp.einsum(
        "hts,she->the", scores, value_heads, preferred_element_type=jnp.float32
    )
    root_mean = jnp.sqrt(jnp.mean(attn * attn, axis=2, keepdims=True) + EPSILON)
    normed = attn / root_mean
    attn_out = normed.astype(jnp.bfloat16).reshape(1, tok_rows, channels)
    upstream = grad_out[0].reshape(tok_rows, head_count, head_size).astype(jnp.float32)
    grad_attn = (
        (upstream - normed * jnp.mean(upstream * normed, axis=2, keepdims=True)) / root_mean
    ).astype(jnp.bfloat16)
    grad_scores = (
        mixing
        * jnp.einsum("the,she->hts", grad_attn, value_heads, preferred_element_type=jnp.float32)
    ).astype(jnp.bfloat16)
    fwd_grad = jnp.einsum(
        "thd,the->hde",
        (shrink * query_heads).astype(jnp.bfloat16),
        grad_attn,
        preferred_element_type=jnp.float32,
    )
    back_grad = jnp.einsum(
        "thd,the->hde",
        (rising * query_heads).astype(jnp.bfloat16),
        grad_attn,
        preferred_element_type=jnp.float32,
    )
    left_gb = scanned(block_decay, fwd_grad, "seq", False).astype(jnp.bfloat16)
    right_gb = scanned(block_decay, back_grad, "seq", True).astype(jnp.bfloat16)
    query_post = rising * jnp.einsum(
        "the,hde->thd", grad_attn, left_b, preferred_element_type=jnp.float32
    )
    query_post = query_post + shrink * jnp.einsum(
        "the,hde->thd", grad_attn, right_b, preferred_element_type=jnp.float32
    )
    query_post = query_post + jnp.einsum(
        "hts,shd->thd", grad_scores, key_heads, preferred_element_type=jnp.float32
    )
    key_post = rising * jnp.einsum(
        "the,hde->thd", value_heads, left_gb, preferred_element_type=jnp.float32
    )
    key_post = key_post + shrink * jnp.einsum(
        "the,hde->thd", value_heads, right_gb, preferred_element_type=jnp.float32
    )
    key_post = key_post + jnp.einsum(
        "hts,thd->shd", grad_scores, query_heads, preferred_element_type=jnp.float32
    )
    value_post = rising * jnp.einsum(
        "thd,hde->the", key_heads, left_gb, preferred_element_type=jnp.float32
    )
    value_post = value_post + shrink * jnp.einsum(
        "thd,hde->the", key_heads, right_gb, preferred_element_type=jnp.float32
    )
    value_post = value_post + jnp.einsum(
        "hts,the->she", scores, grad_attn, preferred_element_type=jnp.float32
    )
    post_grads = jnp.stack(
        [
            query_post.reshape(tok_rows, channels),
            key_post.reshape(tok_rows, channels),
            value_post.reshape(tok_rows, channels),
        ]
    )
    following = shifted(post_grads[:, :rim_rows].astype(jnp.bfloat16), "seq", -1).astype(
        jnp.float32
    )
    grad_query = filter_back(post_grads[0], following[0], conv_kernel[0]).astype(jnp.bfloat16)
    grad_key = filter_back(post_grads[1], following[1], conv_kernel[1]).astype(jnp.bfloat16)
    grad_value = filter_back(post_grads[2], following[2], conv_kernel[2]).astype(jnp.bfloat16)
    kernel_terms = (
        jnp.stack(
            [
                tap_sums(post_grads[which], raw_rows[which], before[which], kernel_width)
                for which in range(3)
            ]
        )
        * grad_scale
    )
    grad_conv = lax.psum(kernel_terms, ("seq", "rep"))
    partial_x = lax.dot_general(
        grad_value,
        lax.all_gather(value_weight, ("seq", "rep"), axis=0, tiled=True),
        (((1,), (1,)), ((), ())),
        preferred_element_type=jnp.float32,
    )
    grad_x = lax.psum_scatter(
        partial_x[None].astype(jnp.bfloat16), "head", scatter_dimension=2, tiled=True
    )
    feature_rows = lax.all_to_all(gathered, ("seq", "rep"), 1, 0, tiled=True)
    grad_value_all = lax.all_gather(grad_value, ("seq", "rep"), axis=0, tiled=True)
    grad_w = (
        lax.dot_general(
            feature_rows,
            grad_value_all,
            (((0,), (0,)), ((), ())),
            preferred_element_type=jnp.float32,
        )
        * grad_scale
    )
    return (attn_out, grad_query[None], grad_key[None], grad_x, grad_w, grad_conv)


def solution(mesh):
    placed = (
        P(("parts", "rep"), "seq", "head"),
        P(("seq", "rep"), "head"),
        P(("parts", "rep"), "seq", "head"),
        P(("parts", "rep"), "seq", "head"),
        P(("parts", "rep"), "seq", "head"),
        P(None, None, "head"),
        P(("parts", "rep"), "head", "seq"),
    )
    return jax.shard_map(
        local,
        mesh=mesh,
        in_specs=placed,
        out_specs=(
            P(("parts", "rep"), "seq", "head"),
            P(("parts", "rep"), "seq", "head"),
            P(("parts", "rep"), "seq", "head"),
            P(("parts", "rep"), "seq", "head"),
            P(("parts", "seq", "rep"), "head"),
            P("parts", None, "head"),
        ),
        check_vma=False,
    )
```

profile of v0, /device:TPU:0, one launch (start us, length us, event | category | flops | bytes accessed | tf_op | source)
XLA Modules:
  0.0 546.2 jit_solution(14763116871213756074)
XLA Ops:
  11.9 75.3 %all-gather.3.cloned.1.call-done = bf16[2048,2048]{1,0:T(8,128)(2,1)} async-done(((bf16[128,2048]{1,0:T(8,128)(2,1)}), bf16[2048,2048]{1,0:T(8,128)(2,1)}) %all-gather.3.cloned.1.call-update) | async-done | bytes 8388624 | tf_op jit(solution)/shard_map/all_gather | solution.py:118
  87.2 4.6 convolution_convert_fusion.1
  92.0 2.2 collective-permute-start.2
  99.4 3.4 collective-permute-start.3
  105.0 4.4 collective-permute-done.9
  111.2 14.4 %collective-permute-start.4 = (f32[16,128,128]{2,1,0:T(8,128)S(1)}, f32[16,128,128]{2,1,0:T(8,128)S(1)}, u32[]{:S(2)}, u32[]{:S(2)}) collective-permute-start(f32[16,128,128]{2,1,0:T(8,128)S(1)} %get-tuple-element.65), channel_id=1, source_target_pairs={{0,4},{2,6},{4,8},{6,10},{8,12},{10,14},{1,5},{3,7},{5,9},{7,11},{... | collective-permute-start | bytes 3145736 | tf_op jit(solution)/shard_map/ppermute | solution.py:13
  125.6 3.6 collective-permute-start
  132.3 14.0 %collective-permute-done.10 = f32[16,128,128]{2,1,0:T(8,128)S(1)} collective-permute-done((f32[16,128,128]{2,1,0:T(8,128)S(1)}, f32[16,128,128]{2,1,0:T(8,128)S(1)}, u32[]{:S(2)}, u32[]{:S(2)}) %collective-permute-start.10) | collective-permute-done | bytes 1048608 | tf_op jit(solution)/shard_map/ppermute | solution.py:13
  150.0 10.6 %collective-permute-start.5 = (f32[16,128,128]{2,1,0:T(8,128)}, f32[16,128,128]{2,1,0:T(8,128)}, u32[]{:S(2)}, u32[]{:S(2)}) collective-permute-start(f32[16,128,128]{2,1,0:T(8,128)} %multiply_add_fusion.10), channel_id=1, source_target_pairs={{0,8},{2,10},{4,12},{6,14},{1,9},{3,11},{5,13},{7,15},{16,24},{18,... | collective-permute-start | bytes 3145736 | tf_op jit(solution)/shard_map/ppermute | solution.py:13
  160.6 2.2 copy.108
  162.8 4.0 collective-permute-start.1
  168.1 13.9 %collective-permute-done.1 = f32[16]{0:T(128)S(1)} collective-permute-done((f32[16]{0:T(128)S(1)}, f32[16]{0:T(128)S(1)}, u32[]{:S(2)}, u32[]{:S(2)}) %collective-permute-start.1) | collective-permute-done | bytes 96 | tf_op jit(solution)/shard_map/ppermute | solution.py:13
  187.1 14.1 %collective-permute-done.11 = f32[16,128,128]{2,1,0:T(8,128)} collective-permute-done((f32[16,128,128]{2,1,0:T(8,128)}, f32[16,128,128]{2,1,0:T(8,128)}, u32[]{:S(2)}, u32[]{:S(2)}) %collective-permute-start.11) | collective-permute-done | bytes 1048608 | tf_op jit(solution)/shard_map/ppermute | solution.py:13
  206.1 3.2 collective-permute-start.6
  213.6 16.0 %collective-permute-start.13 = (f32[16,128,128]{2,1,0:T(8,128)S(1)}, f32[16,128,128]{2,1,0:T(8,128)S(1)}, u32[]{:S(2)}, u32[]{:S(2)}) collective-permute-start(f32[16,128,128]{2,1,0:T(8,128)S(1)} %fusion.53), channel_id=1, source_target_pairs={{0,2},{2,4},{4,6},{6,8},{8,10},{10,12},{12,14},{1,3},{3,5},{5,7},{... | collective-permute-start | bytes 3145736 | tf_op jit(solution)/shard_map/ppermute | solution.py:13
  231.8 4.3 collective-permute-done.17
  238.0 14.6 %collective-permute-start.14 = (f32[16,128,128]{2,1,0:T(8,128)S(1)}, f32[16,128,128]{2,1,0:T(8,128)S(1)}, u32[]{:S(2)}, u32[]{:S(2)}) collective-permute-start(f32[16,128,128]{2,1,0:T(8,128)S(1)} %get-tuple-element.61), channel_id=1, source_target_pairs={{0,4},{2,6},{4,8},{6,10},{8,12},{10,14},{1,5},{3,7},{5,9},{7,11},{... | collective-permute-start | bytes 3145736 | tf_op jit(solution)/shard_map/ppermute | solution.py:13
  253.4 19.0 %collective-permute-done.18 = f32[16,128,128]{2,1,0:T(8,128)S(1)} collective-permute-done((f32[16,128,128]{2,1,0:T(8,128)S(1)}, f32[16,128,128]{2,1,0:T(8,128)S(1)}, u32[]{:S(2)}, u32[]{:S(2)}) %collective-permute-start.18) | collective-permute-done | bytes 1048608 | tf_op jit(solution)/shard_map/ppermute | solution.py:13
  276.2 9.0 %collective-permute-start.15 = (f32[16,128,128]{2,1,0:T(8,128)}, f32[16,128,128]{2,1,0:T(8,128)}, u32[]{:S(2)}, u32[]{:S(2)}) collective-permute-start(f32[16,128,128]{2,1,0:T(8,128)} %multiply_add_fusion.4), channel_id=1, source_target_pairs={{0,8},{2,10},{4,12},{6,14},{1,9},{3,11},{5,13},{7,15},{16,24},{18,... | collective-permute-start | bytes 3145736 | tf_op jit(solution)/shard_map/ppermute | solution.py:13
  287.2 2.0 copy.156
  290.8 36.1 %collective-permute-done.19 = f32[16,128,128]{2,1,0:T(8,128)} collective-permute-done((f32[16,128,128]{2,1,0:T(8,128)}, f32[16,128,128]{2,1,0:T(8,128)}, u32[]{:S(2)}, u32[]{:S(2)}) %collective-permute-start.19) | collective-permute-done | bytes 1048608 | tf_op jit(solution)/shard_map/ppermute | solution.py:13
  331.8 3.2 collective-permute-start.16
  348.1 2.6 copy.159
  350.7 4.3 collective-permute-done.21
  355.0 4.4 multiply_reduce_fusion.3
  361.5 29.8 %all_to_all.19 = bf16[128,16,128]{0,2,1:T(8,128)(2,1)} all-to-all(bf16[128,16,128]{0,2,1:T(8,128)(2,1)} %bitcast.200), channel_id=1, replica_groups=mesh['parts'=2,'seq'=8,'rep'=2,'head'=1] {'seq','rep'}, dimensions={1} | all-to-all | bytes 1048576 | tf_op jit(solution)/shard_map/all_to_all | solution.py:263
  394.7 2.1 copy.139
  398.2 4.1 multiply_reduce_fusion.11
  404.9 8.2 %fusion.1 = bf16[1,128,2048]{2,1,0:T(8,128)(2,1)} fusion(bf16[128,2048]{1,0:T(8,128)(2,1)S(1)} %copy-done.10, bf16[2048,2048]{1,0:T(8,128)(2,1)} %all-gather.3.cloned.1.call-done), kind=kOutput, calls=%fused_computation.4 | convolution fusion | flops 1074003968 | bytes 9437184 | tf_op jit(solution)/shard_map/dot_general | solution.py:254
  413.1 33.6 %all-gather.5.cloned.1.call-done = bf16[2048,2048]{1,0:T(8,128)(2,1)} async-done(((bf16[128,2048]{1,0:T(8,128)(2,1)}), bf16[2048,2048]{1,0:T(8,128)(2,1)}) %all-gather.5.cloned.1.call-update) | async-done | bytes 8388624 | tf_op jit(solution)/shard_map/all_gather | solution.py:264
  446.7 5.8 %fusion = f32[128,2048]{0,1:T(8,128)S(1)} fusion(bf16[2048,2048]{1,0:T(8,128)(2,1)} %all-gather.5.cloned.1.call-done, bf16[2048,128]{1,0:T(8,128)(2,1)S(1)} %bitcast.204), kind=kOutput, calls=%fused_computation.1 | convolution fusion | flops 1074003968 | bytes 9961472 | tf_op jit(solution)/shard_map/dot_general | solution.py:266
  453.8 84.3 %all-reduce.2.cloned.1.call-done = f32[3,4,2048]{2,1,0:T(4,128)} async-done(((f32[3,4,2048]{2,1,0:T(4,128)}), f32[3,4,2048]{2,1,0:T(4,128)}) %all-reduce.2.cloned.1.call-update) | async-done | bytes 98320 | tf_op jit(solution)/shard_map/psum | solution.py:253
  (151 shorter events, 78.4 us)
Async XLA Ops:
  7.2 80.1 %copy-start.15 = (bf16[1,128,2048]{2,1,0:T(8,128)(2,1)S(1)}, bf16[1,128,2048]{2,1,0:T(8,128)(2,1)}, u32[]{:S(2)}) copy-start(bf16[1,128,2048]{2,1,0:T(8,128)(2,1)} %param.7) | copy-start | bytes 1572868
  7.2 80.1 %all-gather.3.cloned.1.call-start = ((), (), s32[]{:S(2)}) async-start(), calls=%async_computation.1 | async-start | bytes 8912896 | tf_op jit(solution)/shard_map/all_gather | solution.py:118
  7.9 438.8 %all-gather.5.cloned.1.call-start = ((), (), s32[]{:S(2)}) async-start(), calls=%async_computation.2 | async-start | bytes 8912896 | tf_op jit(solution)/shard_map/all_gather | solution.py:264
  11.9 83.2 %copy-start.23 = (bf16[1,128,2048]{2,1,0:T(8,128)(2,1)S(1)}, bf16[1,128,2048]{2,1,0:T(8,128)(2,1)}, u32[]{:S(2)}) copy-start(bf16[1,128,2048]{2,1,0:T(8,128)(2,1)} %param.10) | copy-start | bytes 1572868
  11.9 83.2 %copy-start.24 = (bf16[1,128,2048]{2,1,0:T(8,128)(2,1)S(1)}, bf16[1,128,2048]{2,1,0:T(8,128)(2,1)}, u32[]{:S(2)}) copy-start(bf16[1,128,2048]{2,1,0:T(8,128)(2,1)} %param.9) | copy-start | bytes 1572868
  92.0 3.0 collective-permute-start.2
  99.4 5.6 %collective-permute-start.3 = (f32[16,128,128]{2,1,0:T(8,128)S(1)}, f32[16,128,128]{2,1,0:T(8,128)S(1)}, u32[]{:S(2)}, u32[]{:S(2)}) collective-permute-start(f32[16,128,128]{2,1,0:T(8,128)S(1)} %fusion.57), channel_id=1, source_target_pairs={{0,2},{2,4},{4,6},{6,8},{8,10},{10,12},{12,14},{1,3},{3,5},{5,7},{... | collective-permute-start | bytes 3145736 | tf_op jit(solution)/shard_map/ppermute | solution.py:13
  103.1 6.3 %collective-permute-start.9 = (f32[16,128,128]{2,1,0:T(8,128)S(1)}, f32[16,128,128]{2,1,0:T(8,128)S(1)}, u32[]{:S(2)}, u32[]{:S(2)}) collective-permute-start(f32[16,128,128]{2,1,0:T(8,128)S(1)} %fusion.55), channel_id=1, source_target_pairs={{2,0},{4,2},{6,4},{8,6},{10,8},{12,10},{14,12},{3,1},{5,3},{7,5},{... | collective-permute-start | bytes 3145736 | tf_op jit(solution)/shard_map/ppermute | solution.py:13
  109.9 36.4 %collective-permute-start.10 = (f32[16,128,128]{2,1,0:T(8,128)S(1)}, f32[16,128,128]{2,1,0:T(8,128)S(1)}, u32[]{:S(2)}, u32[]{:S(2)}) collective-permute-start(f32[16,128,128]{2,1,0:T(8,128)S(1)} %get-tuple-element.66), channel_id=1, source_target_pairs={{4,0},{6,2},{8,4},{10,6},{12,8},{14,10},{5,1},{7,3},{9,5},{11,7},{... | collective-permute-start | bytes 3145736 | tf_op jit(solution)/shard_map/ppermute | solution.py:13
  111.2 37.6 %collective-permute-start.4 = (f32[16,128,128]{2,1,0:T(8,128)S(1)}, f32[16,128,128]{2,1,0:T(8,128)S(1)}, u32[]{:S(2)}, u32[]{:S(2)}) collective-permute-start(f32[16,128,128]{2,1,0:T(8,128)S(1)} %get-tuple-element.65), channel_id=1, source_target_pairs={{0,4},{2,6},{4,8},{6,10},{8,12},{10,14},{1,5},{3,7},{5,9},{7,11},{... | collective-permute-start | bytes 3145736 | tf_op jit(solution)/shard_map/ppermute | solution.py:13
  125.6 4.9 collective-permute-start
  129.3 3.1 collective-permute-start.7
  147.6 53.6 %collective-permute-start.11 = (f32[16,128,128]{2,1,0:T(8,128)}, f32[16,128,128]{2,1,0:T(8,128)}, u32[]{:S(2)}, u32[]{:S(2)}) collective-permute-start(f32[16,128,128]{2,1,0:T(8,128)} %multiply_add_fusion.7), channel_id=1, source_target_pairs={{8,0},{10,2},{12,4},{14,6},{9,1},{11,3},{13,5},{15,7},{24,16},{26,... | collective-permute-start | bytes 3145736 | tf_op jit(solution)/shard_map/ppermute | solution.py:13
  150.0 54.3 %collective-permute-start.5 = (f32[16,128,128]{2,1,0:T(8,128)}, f32[16,128,128]{2,1,0:T(8,128)}, u32[]{:S(2)}, u32[]{:S(2)}) collective-permute-start(f32[16,128,128]{2,1,0:T(8,128)} %multiply_add_fusion.10), channel_id=1, source_target_pairs={{0,8},{2,10},{4,12},{6,14},{1,9},{3,11},{5,13},{7,15},{16,24},{18,... | collective-permute-start | bytes 3145736 | tf_op jit(solution)/shard_map/ppermute | solution.py:13
  162.8 19.2 %collective-permute-start.1 = (f32[16]{0:T(128)S(1)}, f32[16]{0:T(128)S(1)}, u32[]{:S(2)}, u32[]{:S(2)}) collective-permute-start(f32[16]{0:T(128)S(1)} %get-tuple-element.63), channel_id=1, source_target_pairs={{0,4},{2,6},{4,8},{6,10},{8,12},{10,14},{1,5},{3,7},{5,9},{7,11},{... | collective-permute-start | bytes 200 | tf_op jit(solution)/shard_map/ppermute | solution.py:13
  166.8 15.2 %collective-permute-start.8 = (f32[16]{0:T(128)S(1)}, f32[16]{0:T(128)S(1)}, u32[]{:S(2)}, u32[]{:S(2)}) collective-permute-start(f32[16]{0:T(128)S(1)} %get-tuple-element.64), channel_id=1, source_target_pairs={{4,0},{6,2},{8,4},{10,6},{12,8},{14,10},{5,1},{7,3},{9,5},{11,7},{... | collective-permute-start | bytes 200 | tf_op jit(solution)/shard_map/ppermute | solution.py:13
  202.9 6.9 %collective-permute-start.12 = (bf16[16,128,128]{2,1,0:T(8,128)(2,1)S(1)}, bf16[16,128,128]{2,1,0:T(8,128)(2,1)S(1)}, u32[]{:S(2)}, u32[]{:S(2)}) collective-permute-start(bf16[16,128,128]{2,1,0:T(8,128)(2,1)S(1)} %multiply_add_fusion.6), channel_id=1, source_target_pairs={{2,0},{4,2},{6,4},{8,6},{10,8},{12,10},{14,12},{3,1},{5,3},{7,5},{... | collective-permute-start | bytes 1572872 | tf_op jit(solution)/shard_map/ppermute | solution.py:13
  206.1 4.7 collective-permute-start.6
  212.6 73.1 %copy-start.6 = (bf16[128,16,128]{0,2,1:T(8,128)(2,1)}, bf16[128,16,128]{0,2,1:T(8,128)(2,1)S(1)}, u32[]{:S(2)}) copy-start(bf16[128,16,128]{0,2,1:T(8,128)(2,1)S(1)} %get-tuple-element.36) | copy-start | bytes 1572868
  213.6 18.2 %collective-permute-start.13 = (f32[16,128,128]{2,1,0:T(8,128)S(1)}, f32[16,128,128]{2,1,0:T(8,128)S(1)}, u32[]{:S(2)}, u32[]{:S(2)}) collective-permute-start(f32[16,128,128]{2,1,0:T(8,128)S(1)} %fusion.53), channel_id=1, source_target_pairs={{0,2},{2,4},{4,6},{6,8},{8,10},{10,12},{12,14},{1,3},{3,5},{5,7},{... | collective-permute-start | bytes 3145736 | tf_op jit(solution)/shard_map/ppermute | solution.py:13
  229.6 6.5 %collective-permute-start.17 = (f32[16,128,128]{2,1,0:T(8,128)S(1)}, f32[16,128,128]{2,1,0:T(8,128)S(1)}, u32[]{:S(2)}, u32[]{:S(2)}) collective-permute-start(f32[16,128,128]{2,1,0:T(8,128)S(1)} %fusion.51), channel_id=1, source_target_pairs={{2,0},{4,2},{6,4},{8,6},{10,8},{12,10},{14,12},{3,1},{5,3},{7,5},{... | collective-permute-start | bytes 3145736 | tf_op jit(solution)/shard_map/ppermute | solution.py:13
  236.7 35.7 %collective-permute-start.18 = (f32[16,128,128]{2,1,0:T(8,128)S(1)}, f32[16,128,128]{2,1,0:T(8,128)S(1)}, u32[]{:S(2)}, u32[]{:S(2)}) collective-permute-start(f32[16,128,128]{2,1,0:T(8,128)S(1)} %get-tuple-element.62), channel_id=1, source_target_pairs={{4,0},{6,2},{8,4},{10,6},{12,8},{14,10},{5,1},{7,3},{9,5},{11,7},{... | collective-permute-start | bytes 3145736 | tf_op jit(solution)/shard_map/ppermute | solution.py:13
  238.0 37.1 %collective-permute-start.14 = (f32[16,128,128]{2,1,0:T(8,128)S(1)}, f32[16,128,128]{2,1,0:T(8,128)S(1)}, u32[]{:S(2)}, u32[]{:S(2)}) collective-permute-start(f32[16,128,128]{2,1,0:T(8,128)S(1)} %get-tuple-element.61), channel_id=1, source_target_pairs={{0,4},{2,6},{4,8},{6,10},{8,12},{10,14},{1,5},{3,7},{5,9},{7,11},{... | collective-permute-start | bytes 3145736 | tf_op jit(solution)/shard_map/ppermute | solution.py:13
  253.1 32.1 %copy-start.21 = (bf16[16,128,128]{2,1,0:T(8,128)(2,1)}, bf16[16,128,128]{2,1,0:T(8,128)(2,1)S(1)}, u32[]{:S(2)}) copy-start(bf16[16,128,128]{2,1,0:T(8,128)(2,1)S(1)} %fusion.19) | copy-start | bytes 1572868
  273.6 53.3 %collective-permute-start.19 = (f32[16,128,128]{2,1,0:T(8,128)}, f32[16,128,128]{2,1,0:T(8,128)}, u32[]{:S(2)}, u32[]{:S(2)}) collective-permute-start(f32[16,128,128]{2,1,0:T(8,128)} %multiply_add_fusion.1), channel_id=1, source_target_pairs={{8,0},{10,2},{12,4},{14,6},{9,1},{11,3},{13,5},{15,7},{24,16},{26,... | collective-permute-start | bytes 3145736 | tf_op jit(solution)/shard_map/ppermute | solution.py:13
  276.2 53.9 %collective-permute-start.15 = (f32[16,128,128]{2,1,0:T(8,128)}, f32[16,128,128]{2,1,0:T(8,128)}, u32[]{:S(2)}, u32[]{:S(2)}) collective-permute-start(f32[16,128,128]{2,1,0:T(8,128)} %multiply_add_fusion.4), channel_id=1, source_target_pairs={{0,8},{2,10},{4,12},{6,14},{1,9},{3,11},{5,13},{7,15},{16,24},{18,... | collective-permute-start | bytes 3145736 | tf_op jit(solution)/shard_map/ppermute | solution.py:13
  328.6 7.8 %collective-permute-start.20 = (bf16[16,128,128]{2,1,0:T(8,128)(2,1)S(1)}, bf16[16,128,128]{2,1,0:T(8,128)(2,1)S(1)}, u32[]{:S(2)}, u32[]{:S(2)}) collective-permute-start(bf16[16,128,128]{2,1,0:T(8,128)(2,1)S(1)} %multiply_add_fusion), channel_id=1, source_target_pairs={{2,0},{4,2},{6,4},{8,6},{10,8},{12,10},{14,12},{3,1},{5,3},{7,5},{... | collective-permute-start | bytes 1572872 | tf_op jit(solution)/shard_map/ppermute | solution.py:13
  331.8 5.1 collective-permute-start.16
  346.8 8.2 %collective-permute-start.21 = (bf16[3,3,2048]{2,1,0:T(4,128)(2,1)S(1)}, bf16[3,3,2048]{2,1,0:T(4,128)(2,1)S(1)}, u32[]{:S(2)}, u32[]{:S(2)}) collective-permute-start(bf16[3,3,2048]{2,1,0:T(4,128)(2,1)S(1)} %pad_maximum_fusion.3), channel_id=1, source_target_pairs={{2,0},{4,2},{6,4},{8,6},{10,8},{12,10},{14,12},{3,1},{5,3},{7,5},{... | collective-permute-start | bytes 110600 | tf_op jit(solution)/shard_map/ppermute | solution.py:13
  359.4 178.6 %all-reduce.2.cloned.1.call-start = ((), (), s32[]{:S(2)}) async-start(), calls=%async_computation.3 | async-start | bytes 196608 | tf_op jit(solution)/shard_map/psum | solution.py:253
  361.5 31.9 %copy-start.11 = (f32[128,16,128]{0,2,1:T(8,128)S(1)}, f32[128,16,128]{0,2,1:T(8,128)}, u32[]{:S(2)}) copy-start(f32[128,16,128]{0,2,1:T(8,128)} %get-tuple-element.74) | copy-start | bytes 3145732
  404.9 41.8 %copy-start.25 = (bf16[16,128,128]{2,1,0:T(8,128)(2,1)S(1)}, bf16[16,128,128]{2,1,0:T(8,128)(2,1)}, u32[]{:S(2)}) copy-start(bf16[16,128,128]{2,1,0:T(8,128)(2,1)} %copy.130) | copy-start | bytes 1572868
  (19 other events, 89.3 us)
Sparse Core Ops, SparseCore 0:
  10.2 76.9 all-gather.2
  359.6 87.0 all-gather.4
  450.7 87.3 all-reduce.1
where the time goes:
time: 548 us; the launch traced here: 546 us
  waiting for transfers between devices  309 us (56%)
  starting transfers between devices  98.8 us (18%)
  matrix products  34.2 us (6%)
  other arithmetic  30.6 us (6%)
  blocking collectives  29.8 us (5%)
  local copies, waits for them, and re-layouts  29.6 us (5%)
  between operations  14.4 us (3%)
    ppermute x22, waiting for transfers between devices, shifted(): return lax.ppermute(block, axis, route)  115 us
    ppermute x22, starting transfers between devices, shifted(): return lax.ppermute(block, axis, route)  98.7 us
    psum x1, waiting for transfers between devices, local(): grad_conv = lax.psum(kernel_terms, ('seq', 'rep'))  84.3 us
    all_gather x1, waiting for transfers between devices, local(): lax.all_gather(value_weight, ('seq', 'rep'), axis=0, tiled=True)  75.3 us
    all_gather x1, waiting for transfers between devices, local(): lax.all_gather(grad_value, ('seq', 'rep'), axis=0, tiled=True)  33.6 us
    all_to_all x1, blocking collectives, local(): feature_rows = lax.all_to_all(gathered, ('seq', 'rep'), 1, 0, tiled=True)  29.8 us
    add x10, other arithmetic, chain_join(): following[0][:, None, None] * earlier[1] + following[1]  12.7 us
  transfers between devices with their start and end apart: 25, of which 16 were waited for; matrix products, arithmetic and copies ran while one was open for 12% of the time, Pallas kernels for 0%

commit v1 on v0

--- a/solution.py
+++ b/solution.py
@@ -5,6 +5,28 @@
 from jax.sharding import PartitionSpec as P
 
 EPSILON = 1e-06
+
+
+def joined_along(pieces, dim):
+    pieces = jnp.moveaxis(pieces, 0, dim)
+    shape = pieces.shape
+    return pieces.reshape(*shape[:dim], shape[dim] * shape[dim + 1], *shape[dim + 2 :])
+
+
+def collect(array, axis, dim):
+    size = lax.axis_size(axis)
+    pairs = [(i, (i + 1) % size) for i in range(size)]
+    back = [(b, a) for a, b in pairs]
+    lower, upper = ([], [])
+    for step in range(size - 1):
+        if step % 2 == 0:
+            lower.append(lax.ppermute(lower[-1] if lower else array, axis, pairs))
+        else:
+            upper.append(lax.ppermute(upper[-1] if upper else array, axis, back))
+    parts = jnp.stack([*lower[::-1], array, *upper])
+    shift = lax.axis_index(axis) - len(lower)
+    parts = parts[(jnp.arange(size) - shift) % size]
+    return joined_along(parts, dim)
 
 
 def shifted(block, axis, distance):
@@ -114,9 +136,7 @@
     gathered = lax.all_gather(activations, "head", axis=2, tiled=True)[0]
     columns = gathered
     value_f32 = jnp.dot(
-        columns,
-        lax.all_gather(value_weight, ("seq", "rep"), axis=0, tiled=True),
-        preferred_element_type=jnp.float32,
+        columns, collect(value_weight, ("seq", "rep"), 0), preferred_element_type=jnp.float32
     )
     value_raw = value_f32.astype(jnp.bfloat16)
     before_all = shifted(

time: 548 us -> 682 us (1.24)
  starting transfers between devices: 98.8 us -> 161 us
  waiting for transfers between devices: 309 us -> 344 us
  local copies, waits for them, and re-layouts: 29.6 us -> 57.6 us
    ppermute x0 -> x15, waiting for transfers between devices: none -> 118 us  [the longest x8 65.4 us: collect(): lower.append(lax.ppermute(lower[-1] if lower else array, axis, pairs))]
    all_gather x1, waiting for transfers between devices: 75.3 us -> 0.02 us  [local(): lax.all_gather(value_weight, ('seq', 'rep'), axis=0, tiled=True)]
    ppermute x0 -> x15, starting transfers between devices: none -> 50.5 us  [the longest x8 46.5 us: collect(): lower.append(lax.ppermute(lower[-1] if lower else array, axis, pairs))]
    unnamed x56 -> x63, local copies, waits for them, and re-layouts: 7.99 us -> 26 us
    ppermute x22, starting transfers between devices: 98.7 us -> 110 us  [shifted(): return lax.ppermute(block, axis, route)]
    gather x0 -> x1, local copies, waits for them, and re-layouts: none -> 8.43 us  [collect(): parts = parts[(jnp.arange(size) - shift) % size]]
  transfers between devices with their start and end apart: 25 -> 40, of which waited for: 16 -> 24; matrix products, arithmetic and copies ran while one was open for 12% -> 19% of each run, Pallas kernels for 0% -> 0%
where the time goes in v1:
time: 682 us; the launch traced here: 680 us
  waiting for transfers between devices  344 us (50%)
  starting transfers between devices  161 us (24%)
  local copies, waits for them, and re-layouts  57.6 us (8%)
  matrix products  38.3 us (6%)
  other arithmetic  33.6 us (5%)
  blocking collectives  30.9 us (5%)
  between operations  14.4 us (2%)
    ppermute x22, starting transfers between devices, shifted(): return lax.ppermute(block, axis, route)  110 us
    ppermute x22, waiting for transfers between devices, shifted(): return lax.ppermute(block, axis, route)  109 us
    psum x1, waiting for transfers between devices, local(): grad_conv = lax.psum(kernel_terms, ('seq', 'rep'))  84.3 us
    ppermute x8, waiting for transfers between devices, collect(): lower.append(lax.ppermute(lower[-1] if lower else array, axis, pairs))  65.4 us
    ppermute x7, waiting for transfers between devices, collect(): upper.append(lax.ppermute(upper[-1] if upper else array, axis, back))  52.7 us
    ppermute x8, starting transfers between devices, collect(): lower.append(lax.ppermute(lower[-1] if lower else array, axis, pairs))  46.5 us
    all_gather x1, waiting for transfers between devices, local(): lax.all_gather(grad_value, ('seq', 'rep'), axis=0, tiled=True)  32.6 us
    all_to_all x1, blocking collectives, local(): feature_rows = lax.all_to_all(gathered, ('seq', 'rep'), 1, 0, tiled=True)  30.9 us
  transfers between devices with their start and end apart: 40, of which 24 were waited for; matrix products, arithmetic and copies ran while one was open for 19% of the time, Pallas kernels for 0%

profile of v1, /device:TPU:0, one launch (start us, length us, event | category | flops | bytes accessed | tf_op | source)
XLA Modules:
  0.0 679.6 jit_solution(14391786329677099267)
XLA Ops:
  10.2 11.5 %collective-permute-done.2 = bf16[128,2048]{1,0:T(8,128)(2,1)S(1)} collective-permute-done((bf16[128,2048]{1,0:T(8,128)(2,1)}, bf16[128,2048]{1,0:T(8,128)(2,1)S(1)}, u32[]{:S(2)}, u32[]{:S(2)}) %collective-permute-start.2) | collective-permute-done | bytes 524320 | tf_op jit(solution)/shard_map/ppermute | solution.py:23
  26.2 15.9 %collective-permute-done.3 = bf16[128,2048]{1,0:T(8,128)(2,1)S(1)} collective-permute-done((bf16[128,2048]{1,0:T(8,128)(2,1)S(1)}, bf16[128,2048]{1,0:T(8,128)(2,1)S(1)}, u32[]{:S(2)}, u32[]{:S(2)}) %collective-permute-start.3) | collective-permute-done | bytes 524320 | tf_op jit(solution)/shard_map/ppermute | solution.py:23
  44.5 10.1 %collective-permute-done.10 = bf16[128,2048]{1,0:T(8,128)(2,1)S(1)} collective-permute-done((bf16[128,2048]{1,0:T(8,128)(2,1)}, bf16[128,2048]{1,0:T(8,128)(2,1)S(1)}, u32[]{:S(2)}, u32[]{:S(2)}) %collective-permute-start.10) | collective-permute-done | bytes 524320 | tf_op jit(solution)/shard_map/ppermute | solution.py:25
  56.9 8.0 %collective-permute-start.5 = (bf16[128,2048]{1,0:T(8,128)(2,1)S(1)}, bf16[128,2048]{1,0:T(8,128)(2,1)S(1)}, u32[]{:S(2)}, u32[]{:S(2)}) collective-permute-start(bf16[128,2048]{1,0:T(8,128)(2,1)S(1)} %collective-permute-done.4), channel_id=1, source_target_pairs={{0,1},{1,2},{2,3},{3,4},{4,5},{5,6},{6,7},{7,8},{8,9},{9,10},{10,1... | collective-permute-start | bytes 1572872 | tf_op jit(solution)/shard_map/ppermute | solution.py:23
  64.8 13.5 %collective-permute-done.11 = bf16[128,2048]{1,0:T(8,128)(2,1)S(1)} collective-permute-done((bf16[128,2048]{1,0:T(8,128)(2,1)S(1)}, bf16[128,2048]{1,0:T(8,128)(2,1)S(1)}, u32[]{:S(2)}, u32[]{:S(2)}) %collective-permute-start.11) | collective-permute-done | bytes 524320 | tf_op jit(solution)/shard_map/ppermute | solution.py:25
  78.4 8.9 %collective-permute-start.6 = (bf16[128,2048]{1,0:T(8,128)(2,1)S(1)}, bf16[128,2048]{1,0:T(8,128)(2,1)S(1)}, u32[]{:S(2)}, u32[]{:S(2)}) collective-permute-start(bf16[128,2048]{1,0:T(8,128)(2,1)S(1)} %collective-permute-done.5), channel_id=1, source_target_pairs={{0,1},{1,2},{2,3},{3,4},{4,5},{5,6},{6,7},{7,8},{8,9},{9,10},{10,1... | collective-permute-start | bytes 1572872 | tf_op jit(solution)/shard_map/ppermute | solution.py:23
  87.3 13.5 %collective-permute-done.12 = bf16[128,2048]{1,0:T(8,128)(2,1)S(1)} collective-permute-done((bf16[128,2048]{1,0:T(8,128)(2,1)S(1)}, bf16[128,2048]{1,0:T(8,128)(2,1)S(1)}, u32[]{:S(2)}, u32[]{:S(2)}) %collective-permute-start.12) | collective-permute-done | bytes 524320 | tf_op jit(solution)/shard_map/ppermute | solution.py:25
  101.6 13.8 %collective-permute-start.7 = (bf16[128,2048]{1,0:T(8,128)(2,1)S(1)}, bf16[128,2048]{1,0:T(8,128)(2,1)}, u32[]{:S(2)}, u32[]{:S(2)}) collective-permute-start(bf16[128,2048]{1,0:T(8,128)(2,1)S(1)} %collective-permute-done.6), channel_id=1, source_target_pairs={{0,1},{1,2},{2,3},{3,4},{4,5},{5,6},{6,7},{7,8},{8,9},{9,10},{10,1... | collective-permute-start | bytes 1572872 | tf_op jit(solution)/shard_map/ppermute | solution.py:23
  115.4 9.1 %collective-permute-done.13 = bf16[128,2048]{1,0:T(8,128)(2,1)} collective-permute-done((bf16[128,2048]{1,0:T(8,128)(2,1)S(1)}, bf16[128,2048]{1,0:T(8,128)(2,1)}, u32[]{:S(2)}, u32[]{:S(2)}) %collective-permute-start.13) | collective-permute-done | bytes 524320 | tf_op jit(solution)/shard_map/ppermute | solution.py:25
  124.5 8.8 %collective-permute-done.7 = bf16[128,2048]{1,0:T(8,128)(2,1)} collective-permute-done((bf16[128,2048]{1,0:T(8,128)(2,1)S(1)}, bf16[128,2048]{1,0:T(8,128)(2,1)}, u32[]{:S(2)}, u32[]{:S(2)}) %collective-permute-start.7) | collective-permute-done | bytes 524320 | tf_op jit(solution)/shard_map/ppermute | solution.py:23
  140.6 13.4 %collective-permute-done.8 = bf16[128,2048]{1,0:T(8,128)(2,1)} collective-permute-done((bf16[128,2048]{1,0:T(8,128)(2,1)}, bf16[128,2048]{1,0:T(8,128)(2,1)}, u32[]{:S(2)}, u32[]{:S(2)}) %collective-permute-start.8) | collective-permute-done | bytes 524320 | tf_op jit(solution)/shard_map/ppermute | solution.py:23
  154.1 5.4 collective-permute-start.9
  160.6 6.5 collective-permute-done.15
  167.1 13.6 %collective-permute-done.9 = bf16[128,2048]{1,0:T(8,128)(2,1)S(1)} collective-permute-done((bf16[128,2048]{1,0:T(8,128)(2,1)}, bf16[128,2048]{1,0:T(8,128)(2,1)S(1)}, u32[]{:S(2)}, u32[]{:S(2)}) %collective-permute-start.9) | collective-permute-done | bytes 524320 | tf_op jit(solution)/shard_map/ppermute | solution.py:23
  200.5 8.4 %gather_fusion = bf16[16,128,2048]{2,1,0:T(8,128)(2,1)} fusion(bf16[16,128,2048]{2,1,0:T(8,128)(2,1)} %bitcast_dynamic-update-slice_fusion, s32[1024]{0:T(1024)S(1)} %pad_clamp_fusion), kind=kCustom, calls=%fused_computation | custom fusion | bytes 16777280 | tf_op jit(solution)/shard_map/gather | solution.py:28
  208.9 4.7 fusion.2
  213.8 15.7 %collective-permute-start.17 = (bf16[3,3,2048]{2,1,0:T(4,128)(2,1)S(1)}, bf16[3,3,2048]{2,1,0:T(4,128)(2,1)S(1)}, u32[]{:S(2)}, u32[]{:S(2)}) collective-permute-start(bf16[3,3,2048]{2,1,0:T(4,128)(2,1)S(1)} %pad_maximum_fusion.5), channel_id=1, source_target_pairs={{0,2},{2,4},{4,6},{6,8},{8,10},{10,12},{12,14},{1,3},{3,5},{5,7},{... | collective-permute-start | bytes 110600 | tf_op jit(solution)/shard_map/ppermute | solution.py:35
  244.3 16.6 %collective-permute-start.19 = (f32[16,128,128]{2,1,0:T(8,128)S(1)}, f32[16,128,128]{2,1,0:T(8,128)S(1)}, u32[]{:S(2)}, u32[]{:S(2)}) collective-permute-start(f32[16,128,128]{2,1,0:T(8,128)S(1)} %get-tuple-element.65), channel_id=1, source_target_pairs={{0,4},{2,6},{4,8},{6,10},{8,12},{10,14},{1,5},{3,7},{5,9},{7,11},{... | collective-permute-start | bytes 3145736 | tf_op jit(solution)/shard_map/ppermute | solution.py:35
  267.6 14.4 %collective-permute-done.25 = f32[16,128,128]{2,1,0:T(8,128)S(1)} collective-permute-done((f32[16,128,128]{2,1,0:T(8,128)S(1)}, f32[16,128,128]{2,1,0:T(8,128)S(1)}, u32[]{:S(2)}, u32[]{:S(2)}) %collective-permute-start.25) | collective-permute-done | bytes 1048608 | tf_op jit(solution)/shard_map/ppermute | solution.py:35
  285.7 7.5 %collective-permute-start.20 = (f32[16,128,128]{2,1,0:T(8,128)}, f32[16,128,128]{2,1,0:T(8,128)}, u32[]{:S(2)}, u32[]{:S(2)}) collective-permute-start(f32[16,128,128]{2,1,0:T(8,128)} %multiply_add_fusion.10), channel_id=1, source_target_pairs={{0,8},{2,10},{4,12},{6,14},{1,9},{3,11},{5,13},{7,15},{16,24},{18,... | collective-permute-start | bytes 3145736 | tf_op jit(solution)/shard_map/ppermute | solution.py:35
  301.2 13.9 %collective-permute-done.1 = f32[16]{0:T(128)S(1)} collective-permute-done((f32[16]{0:T(128)S(1)}, f32[16]{0:T(128)S(1)}, u32[]{:S(2)}, u32[]{:S(2)}) %collective-permute-start.1) | collective-permute-done | bytes 96 | tf_op jit(solution)/shard_map/ppermute | solution.py:35
  320.2 13.9 %collective-permute-done.26 = f32[16,128,128]{2,1,0:T(8,128)} collective-permute-done((f32[16,128,128]{2,1,0:T(8,128)}, f32[16,128,128]{2,1,0:T(8,128)}, u32[]{:S(2)}, u32[]{:S(2)}) %collective-permute-start.26) | collective-permute-done | bytes 1048608 | tf_op jit(solution)/shard_map/ppermute | solution.py:35
  348.2 16.3 %collective-permute-start.28 = (f32[16,128,128]{2,1,0:T(8,128)S(1)}, f32[16,128,128]{2,1,0:T(8,128)S(1)}, u32[]{:S(2)}, u32[]{:S(2)}) collective-permute-start(f32[16,128,128]{2,1,0:T(8,128)S(1)} %fusion.54), channel_id=1, source_target_pairs={{0,2},{2,4},{4,6},{6,8},{8,10},{10,12},{12,14},{1,3},{3,5},{5,7},{... | collective-permute-start | bytes 3145736 | tf_op jit(solution)/shard_map/ppermute | solution.py:35
  368.6 16.9 %collective-permute-start.29 = (f32[16,128,128]{2,1,0:T(8,128)S(1)}, f32[16,128,128]{2,1,0:T(8,128)S(1)}, u32[]{:S(2)}, u32[]{:S(2)}) collective-permute-start(f32[16,128,128]{2,1,0:T(8,128)S(1)} %get-tuple-element.61), channel_id=1, source_target_pairs={{0,4},{2,6},{4,8},{6,10},{8,12},{10,14},{1,5},{3,7},{5,9},{7,11},{... | collective-permute-start | bytes 3145736 | tf_op jit(solution)/shard_map/ppermute | solution.py:35
  386.4 20.4 %collective-permute-done.33 = f32[16,128,128]{2,1,0:T(8,128)S(1)} collective-permute-done((f32[16,128,128]{2,1,0:T(8,128)S(1)}, f32[16,128,128]{2,1,0:T(8,128)S(1)}, u32[]{:S(2)}, u32[]{:S(2)}) %collective-permute-start.33) | collective-permute-done | bytes 1048608 | tf_op jit(solution)/shard_map/ppermute | solution.py:35
  410.5 7.5 %collective-permute-start.30 = (f32[16,128,128]{2,1,0:T(8,128)}, f32[16,128,128]{2,1,0:T(8,128)}, u32[]{:S(2)}, u32[]{:S(2)}) collective-permute-start(f32[16,128,128]{2,1,0:T(8,128)} %multiply_add_fusion.4), channel_id=1, source_target_pairs={{0,8},{2,10},{4,12},{6,14},{1,9},{3,11},{5,13},{7,15},{16,24},{18,... | collective-permute-start | bytes 3145736 | tf_op jit(solution)/shard_map/ppermute | solution.py:35
  423.6 34.6 %collective-permute-done.34 = f32[16,128,128]{2,1,0:T(8,128)} collective-permute-done((f32[16,128,128]{2,1,0:T(8,128)}, f32[16,128,128]{2,1,0:T(8,128)}, u32[]{:S(2)}, u32[]{:S(2)}) %collective-permute-start.34) | collective-permute-done | bytes 1048608 | tf_op jit(solution)/shard_map/ppermute | solution.py:35
  492.6 30.9 %all_to_all.19 = bf16[128,16,128]{0,2,1:T(8,128)(2,1)S(1)} all-to-all(bf16[128,16,128]{0,2,1:T(8,128)(2,1)S(1)} %bitcast.238), channel_id=1, replica_groups=mesh['parts'=2,'seq'=8,'rep'=2,'head'=1] {'seq','rep'}, dimensions={1} | all-to-all | bytes 1048576 | tf_op jit(solution)/shard_map/all_to_all | solution.py:283
  540.5 7.1 %fusion.1 = bf16[1,128,2048]{2,1,0:T(8,128)(2,1)} fusion(bf16[128,2048]{1,0:T(8,128)(2,1)S(1)} %copy-done.8, bf16[2048,2048]{1,0:T(8,128)(2,1)} %all-gather.3.cloned.1.call-done), kind=kOutput, calls=%fused_computation.5 | convolution fusion | flops 1074003968 | bytes 9437184 | tf_op jit(solution)/shard_map/dot_general | solution.py:274
  547.5 32.6 %all-gather.5.cloned.1.call-done = bf16[2048,2048]{1,0:T(8,128)(2,1)} async-done(((bf16[128,2048]{1,0:T(8,128)(2,1)}), bf16[2048,2048]{1,0:T(8,128)(2,1)}) %all-gather.5.cloned.1.call-update) | async-done | bytes 8388624 | tf_op jit(solution)/shard_map/all_gather | solution.py:284
  580.1 5.8 fusion
  587.2 84.3 %all-reduce.2.cloned.1.call-done = f32[3,4,2048]{2,1,0:T(4,128)} async-done(((f32[3,4,2048]{2,1,0:T(4,128)}), f32[3,4,2048]{2,1,0:T(4,128)}) %all-reduce.2.cloned.1.call-update) | async-done | bytes 98320 | tf_op jit(solution)/shard_map/psum | solution.py:273
  (192 shorter events, 161.7 us)
Async XLA Ops:
  7.2 533.3 %all-gather.3.cloned.1.call-start = ((), (), s32[]{:S(2)}) async-start(), calls=%async_computation.1 | async-start | bytes 8912896 | tf_op jit(solution)/shard_map/all_gather | solution.py:276
  7.2 14.5 %collective-permute-start.2 = (bf16[128,2048]{1,0:T(8,128)(2,1)}, bf16[128,2048]{1,0:T(8,128)(2,1)S(1)}, u32[]{:S(2)}, u32[]{:S(2)}) collective-permute-start(bf16[128,2048]{1,0:T(8,128)(2,1)} %param.8), channel_id=1, source_target_pairs={{0,1},{1,2},{2,3},{3,4},{4,5},{5,6},{6,7},{7,8},{8,9},{9,10},{10,1... | collective-permute-start | bytes 1572872 | tf_op jit(solution)/shard_map/ppermute | solution.py:23
  21.7 20.3 %collective-permute-start.3 = (bf16[128,2048]{1,0:T(8,128)(2,1)S(1)}, bf16[128,2048]{1,0:T(8,128)(2,1)S(1)}, u32[]{:S(2)}, u32[]{:S(2)}) collective-permute-start(bf16[128,2048]{1,0:T(8,128)(2,1)S(1)} %collective-permute-done.2), channel_id=1, source_target_pairs={{0,1},{1,2},{2,3},{3,4},{4,5},{5,6},{6,7},{7,8},{8,9},{9,10},{10,1... | collective-permute-start | bytes 1572872 | tf_op jit(solution)/shard_map/ppermute | solution.py:23
  24.1 30.5 %collective-permute-start.10 = (bf16[128,2048]{1,0:T(8,128)(2,1)}, bf16[128,2048]{1,0:T(8,128)(2,1)S(1)}, u32[]{:S(2)}, u32[]{:S(2)}) collective-permute-start(bf16[128,2048]{1,0:T(8,128)(2,1)} %param.8), channel_id=1, source_target_pairs={{1,0},{2,1},{3,2},{4,3},{5,4},{6,5},{7,6},{8,7},{9,8},{10,9},{11,1... | collective-permute-start | bytes 1572872 | tf_op jit(solution)/shard_map/ppermute | solution.py:25
  42.1 14.8 %collective-permute-start.4 = (bf16[128,2048]{1,0:T(8,128)(2,1)S(1)}, bf16[128,2048]{1,0:T(8,128)(2,1)S(1)}, u32[]{:S(2)}, u32[]{:S(2)}) collective-permute-start(bf16[128,2048]{1,0:T(8,128)(2,1)S(1)} %collective-permute-done.3), channel_id=1, source_target_pairs={{0,1},{1,2},{2,3},{3,4},{4,5},{5,6},{6,7},{7,8},{8,9},{9,10},{10,1... | collective-permute-start | bytes 1572872 | tf_op jit(solution)/shard_map/ppermute | solution.py:23
  54.6 23.7 %collective-permute-start.11 = (bf16[128,2048]{1,0:T(8,128)(2,1)S(1)}, bf16[128,2048]{1,0:T(8,128)(2,1)S(1)}, u32[]{:S(2)}, u32[]{:S(2)}) collective-permute-start(bf16[128,2048]{1,0:T(8,128)(2,1)S(1)} %collective-permute-done.10), channel_id=1, source_target_pairs={{1,0},{2,1},{3,2},{4,3},{5,4},{6,5},{7,6},{8,7},{9,8},{10,9},{11,1... | collective-permute-start | bytes 1572872 | tf_op jit(solution)/shard_map/ppermute | solution.py:25
  56.9 21.5 %collective-permute-start.5 = (bf16[128,2048]{1,0:T(8,128)(2,1)S(1)}, bf16[128,2048]{1,0:T(8,128)(2,1)S(1)}, u32[]{:S(2)}, u32[]{:S(2)}) collective-permute-start(bf16[128,2048]{1,0:T(8,128)(2,1)S(1)} %collective-permute-done.4), channel_id=1, source_target_pairs={{0,1},{1,2},{2,3},{3,4},{4,5},{5,6},{6,7},{7,8},{8,9},{9,10},{10,1... | collective-permute-start | bytes 1572872 | tf_op jit(solution)/shard_map/ppermute | solution.py:23
  78.4 22.5 %collective-permute-start.12 = (bf16[128,2048]{1,0:T(8,128)(2,1)S(1)}, bf16[128,2048]{1,0:T(8,128)(2,1)S(1)}, u32[]{:S(2)}, u32[]{:S(2)}) collective-permute-start(bf16[128,2048]{1,0:T(8,128)(2,1)S(1)} %collective-permute-done.11), channel_id=1, source_target_pairs={{1,0},{2,1},{3,2},{4,3},{5,4},{6,5},{7,6},{8,7},{9,8},{10,9},{11,1... | collective-permute-start | bytes 1572872 | tf_op jit(solution)/shard_map/ppermute | solution.py:25
  78.4 23.3 %collective-permute-start.6 = (bf16[128,2048]{1,0:T(8,128)(2,1)S(1)}, bf16[128,2048]{1,0:T(8,128)(2,1)S(1)}, u32[]{:S(2)}, u32[]{:S(2)}) collective-permute-start(bf16[128,2048]{1,0:T(8,128)(2,1)S(1)} %collective-permute-done.5), channel_id=1, source_target_pairs={{0,1},{1,2},{2,3},{3,4},{4,5},{5,6},{6,7},{7,8},{8,9},{9,10},{10,1... | collective-permute-start | bytes 1572872 | tf_op jit(solution)/shard_map/ppermute | solution.py:23
  101.6 22.9 %collective-permute-start.13 = (bf16[128,2048]{1,0:T(8,128)(2,1)S(1)}, bf16[128,2048]{1,0:T(8,128)(2,1)}, u32[]{:S(2)}, u32[]{:S(2)}) collective-permute-start(bf16[128,2048]{1,0:T(8,128)(2,1)S(1)} %collective-permute-done.12), channel_id=1, source_target_pairs={{1,0},{2,1},{3,2},{4,3},{5,4},{6,5},{7,6},{8,7},{9,8},{10,9},{11,1... | collective-permute-start | bytes 1572872 | tf_op jit(solution)/shard_map/ppermute | solution.py:25
  101.6 31.7 %collective-permute-start.7 = (bf16[128,2048]{1,0:T(8,128)(2,1)S(1)}, bf16[128,2048]{1,0:T(8,128)(2,1)}, u32[]{:S(2)}, u32[]{:S(2)}) collective-permute-start(bf16[128,2048]{1,0:T(8,128)(2,1)S(1)} %collective-permute-done.6), channel_id=1, source_target_pairs={{0,1},{1,2},{2,3},{3,4},{4,5},{5,6},{6,7},{7,8},{8,9},{9,10},{10,1... | collective-permute-start | bytes 1572872 | tf_op jit(solution)/shard_map/ppermute | solution.py:23
  124.5 14.3 %collective-permute-start.14 = (bf16[128,2048]{1,0:T(8,128)(2,1)}, bf16[128,2048]{1,0:T(8,128)(2,1)}, u32[]{:S(2)}, u32[]{:S(2)}) collective-permute-start(bf16[128,2048]{1,0:T(8,128)(2,1)} %collective-permute-done.13), channel_id=1, source_target_pairs={{1,0},{2,1},{3,2},{4,3},{5,4},{6,5},{7,6},{8,7},{9,8},{10,9},{11,1... | collective-permute-start | bytes 1572872 | tf_op jit(solution)/shard_map/ppermute | solution.py:25
  133.3 20.7 %collective-permute-start.8 = (bf16[128,2048]{1,0:T(8,128)(2,1)}, bf16[128,2048]{1,0:T(8,128)(2,1)}, u32[]{:S(2)}, u32[]{:S(2)}) collective-permute-start(bf16[128,2048]{1,0:T(8,128)(2,1)} %collective-permute-done.7), channel_id=1, source_target_pairs={{0,1},{1,2},{2,3},{3,4},{4,5},{5,6},{6,7},{7,8},{8,9},{9,10},{10,1... | collective-permute-start | bytes 1572872 | tf_op jit(solution)/shard_map/ppermute | solution.py:23
  135.9 444.2 %all-gather.5.cloned.1.call-start = ((), (), s32[]{:S(2)}) async-start(), calls=%async_computation.2 | async-start | bytes 8912896 | tf_op jit(solution)/shard_map/all_gather | solution.py:284
  138.7 28.4 %collective-permute-start.15 = (bf16[128,2048]{1,0:T(8,128)(2,1)}, bf16[128,2048]{1,0:T(8,128)(2,1)S(1)}, u32[]{:S(2)}, u32[]{:S(2)}) collective-permute-start(bf16[128,2048]{1,0:T(8,128)(2,1)} %collective-permute-done.14), channel_id=1, source_target_pairs={{1,0},{2,1},{3,2},{4,3},{5,4},{6,5},{7,6},{8,7},{9,8},{10,9},{11,1... | collective-permute-start | bytes 1572872 | tf_op jit(solution)/shard_map/ppermute | solution.py:25
  154.1 26.7 %collective-permute-start.9 = (bf16[128,2048]{1,0:T(8,128)(2,1)}, bf16[128,2048]{1,0:T(8,128)(2,1)S(1)}, u32[]{:S(2)}, u32[]{:S(2)}) collective-permute-start(bf16[128,2048]{1,0:T(8,128)(2,1)} %collective-permute-done.8), channel_id=1, source_target_pairs={{0,1},{1,2},{2,3},{3,4},{4,5},{5,6},{6,7},{7,8},{8,9},{9,10},{10,1... | collective-permute-start | bytes 1572872 | tf_op jit(solution)/shard_map/ppermute | solution.py:23
  167.1 32.5 %collective-permute-start.16 = (bf16[128,2048]{1,0:T(8,128)(2,1)S(1)}, bf16[128,2048]{1,0:T(8,128)(2,1)S(1)}, u32[]{:S(2)}, u32[]{:S(2)}) collective-permute-start(bf16[128,2048]{1,0:T(8,128)(2,1)S(1)} %collective-permute-done.15), channel_id=1, source_target_pairs={{1,0},{2,1},{3,2},{4,3},{5,4},{6,5},{7,6},{8,7},{9,8},{10,9},{11,1... | collective-permute-start | bytes 1572872 | tf_op jit(solution)/shard_map/ppermute | solution.py:25
  213.8 16.6 %collective-permute-start.17 = (bf16[3,3,2048]{2,1,0:T(4,128)(2,1)S(1)}, bf16[3,3,2048]{2,1,0:T(4,128)(2,1)S(1)}, u32[]{:S(2)}, u32[]{:S(2)}) collective-permute-start(bf16[3,3,2048]{2,1,0:T(4,128)(2,1)S(1)} %pad_maximum_fusion.5), channel_id=1, source_target_pairs={{0,2},{2,4},{4,6},{6,8},{8,10},{10,12},{12,14},{1,3},{3,5},{5,7},{... | collective-permute-start | bytes 110600 | tf_op jit(solution)/shard_map/ppermute | solution.py:35
  243.0 39.1 %collective-permute-start.25 = (f32[16,128,128]{2,1,0:T(8,128)S(1)}, f32[16,128,128]{2,1,0:T(8,128)S(1)}, u32[]{:S(2)}, u32[]{:S(2)}) collective-permute-start(f32[16,128,128]{2,1,0:T(8,128)S(1)} %get-tuple-element.66), channel_id=1, source_target_pairs={{4,0},{6,2},{8,4},{10,6},{12,8},{14,10},{5,1},{7,3},{9,5},{11,7},{... | collective-permute-start | bytes 3145736 | tf_op jit(solution)/shard_map/ppermute | solution.py:35
  244.3 40.3 %collective-permute-start.19 = (f32[16,128,128]{2,1,0:T(8,128)S(1)}, f32[16,128,128]{2,1,0:T(8,128)S(1)}, u32[]{:S(2)}, u32[]{:S(2)}) collective-permute-start(f32[16,128,128]{2,1,0:T(8,128)S(1)} %get-tuple-element.65), channel_id=1, source_target_pairs={{0,4},{2,6},{4,8},{6,10},{8,12},{10,14},{1,5},{3,7},{5,9},{7,11},{... | collective-permute-start | bytes 3145736 | tf_op jit(solution)/shard_map/ppermute | solution.py:35
  283.2 50.9 %collective-permute-start.26 = (f32[16,128,128]{2,1,0:T(8,128)}, f32[16,128,128]{2,1,0:T(8,128)}, u32[]{:S(2)}, u32[]{:S(2)}) collective-permute-start(f32[16,128,128]{2,1,0:T(8,128)} %multiply_add_fusion.7), channel_id=1, source_target_pairs={{8,0},{10,2},{12,4},{14,6},{9,1},{11,3},{13,5},{15,7},{24,16},{26,... | collective-permute-start | bytes 3145736 | tf_op jit(solution)/shard_map/ppermute | solution.py:35
  285.7 51.5 %collective-permute-start.20 = (f32[16,128,128]{2,1,0:T(8,128)}, f32[16,128,128]{2,1,0:T(8,128)}, u32[]{:S(2)}, u32[]{:S(2)}) collective-permute-start(f32[16,128,128]{2,1,0:T(8,128)} %multiply_add_fusion.10), channel_id=1, source_target_pairs={{0,8},{2,10},{4,12},{6,14},{1,9},{3,11},{5,13},{7,15},{16,24},{18,... | collective-permute-start | bytes 3145736 | tf_op jit(solution)/shard_map/ppermute | solution.py:35
  295.4 19.7 %collective-permute-start.1 = (f32[16]{0:T(128)S(1)}, f32[16]{0:T(128)S(1)}, u32[]{:S(2)}, u32[]{:S(2)}) collective-permute-start(f32[16]{0:T(128)S(1)} %get-tuple-element.63), channel_id=1, source_target_pairs={{0,4},{2,6},{4,8},{6,10},{8,12},{10,14},{1,5},{3,7},{5,9},{7,11},{... | collective-permute-start | bytes 200 | tf_op jit(solution)/shard_map/ppermute | solution.py:35
  299.9 15.2 %collective-permute-start.23 = (f32[16]{0:T(128)S(1)}, f32[16]{0:T(128)S(1)}, u32[]{:S(2)}, u32[]{:S(2)}) collective-permute-start(f32[16]{0:T(128)S(1)} %get-tuple-element.64), channel_id=1, source_target_pairs={{4,0},{6,2},{8,4},{10,6},{12,8},{14,10},{5,1},{7,3},{9,5},{11,7},{... | collective-permute-start | bytes 200 | tf_op jit(solution)/shard_map/ppermute | solution.py:35
  346.8 17.9 %collective-permute-start.32 = (f32[16,128,128]{2,1,0:T(8,128)S(1)}, f32[16,128,128]{2,1,0:T(8,128)S(1)}, u32[]{:S(2)}, u32[]{:S(2)}) collective-permute-start(f32[16,128,128]{2,1,0:T(8,128)S(1)} %fusion.52), channel_id=1, source_target_pairs={{2,0},{4,2},{6,4},{8,6},{10,8},{12,10},{14,12},{3,1},{5,3},{7,5},{... | collective-permute-start | bytes 3145736 | tf_op jit(solution)/shard_map/ppermute | solution.py:35
  348.2 18.6 %collective-permute-start.28 = (f32[16,128,128]{2,1,0:T(8,128)S(1)}, f32[16,128,128]{2,1,0:T(8,128)S(1)}, u32[]{:S(2)}, u32[]{:S(2)}) collective-permute-start(f32[16,128,128]{2,1,0:T(8,128)S(1)} %fusion.54), channel_id=1, source_target_pairs={{0,2},{2,4},{4,6},{6,8},{8,10},{10,12},{12,14},{1,3},{3,5},{5,7},{... | collective-permute-start | bytes 3145736 | tf_op jit(solution)/shard_map/ppermute | solution.py:35
  367.3 39.5 %collective-permute-start.33 = (f32[16,128,128]{2,1,0:T(8,128)S(1)}, f32[16,128,128]{2,1,0:T(8,128)S(1)}, u32[]{:S(2)}, u32[]{:S(2)}) collective-permute-start(f32[16,128,128]{2,1,0:T(8,128)S(1)} %get-tuple-element.62), channel_id=1, source_target_pairs={{4,0},{6,2},{8,4},{10,6},{12,8},{14,10},{5,1},{7,3},{9,5},{11,7},{... | collective-permute-start | bytes 3145736 | tf_op jit(solution)/shard_map/ppermute | solution.py:35
  368.6 40.7 %collective-permute-start.29 = (f32[16,128,128]{2,1,0:T(8,128)S(1)}, f32[16,128,128]{2,1,0:T(8,128)S(1)}, u32[]{:S(2)}, u32[]{:S(2)}) collective-permute-start(f32[16,128,128]{2,1,0:T(8,128)S(1)} %get-tuple-element.61), channel_id=1, source_target_pairs={{0,4},{2,6},{4,8},{6,10},{8,12},{10,14},{1,5},{3,7},{5,9},{7,11},{... | collective-permute-start | bytes 3145736 | tf_op jit(solution)/shard_map/ppermute | solution.py:35
  408.1 50.1 %collective-permute-start.34 = (f32[16,128,128]{2,1,0:T(8,128)}, f32[16,128,128]{2,1,0:T(8,128)}, u32[]{:S(2)}, u32[]{:S(2)}) collective-permute-start(f32[16,128,128]{2,1,0:T(8,128)} %multiply_add_fusion.1), channel_id=1, source_target_pairs={{8,0},{10,2},{12,4},{14,6},{9,1},{11,3},{13,5},{15,7},{24,16},{26,... | collective-permute-start | bytes 3145736 | tf_op jit(solution)/shard_map/ppermute | solution.py:35
  410.5 50.7 %collective-permute-start.30 = (f32[16,128,128]{2,1,0:T(8,128)}, f32[16,128,128]{2,1,0:T(8,128)}, u32[]{:S(2)}, u32[]{:S(2)}) collective-permute-start(f32[16,128,128]{2,1,0:T(8,128)} %multiply_add_fusion.4), channel_id=1, source_target_pairs={{0,8},{2,10},{4,12},{6,14},{1,9},{3,11},{5,13},{7,15},{16,24},{18,... | collective-permute-start | bytes 3145736 | tf_op jit(solution)/shard_map/ppermute | solution.py:35
  459.9 8.6 %collective-permute-start.35 = (bf16[16,128,128]{2,1,0:T(8,128)(2,1)S(1)}, bf16[16,128,128]{2,1,0:T(8,128)(2,1)S(1)}, u32[]{:S(2)}, u32[]{:S(2)}) collective-permute-start(bf16[16,128,128]{2,1,0:T(8,128)(2,1)S(1)} %multiply_add_fusion), channel_id=1, source_target_pairs={{2,0},{4,2},{6,4},{8,6},{10,8},{12,10},{14,12},{3,1},{5,3},{7,5},{... | collective-permute-start | bytes 1572872 | tf_op jit(solution)/shard_map/ppermute | solution.py:35
  491.2 180.3 %all-reduce.2.cloned.1.call-start = ((), (), s32[]{:S(2)}) async-start(), calls=%async_computation.3 | async-start | bytes 196608 | tf_op jit(solution)/shard_map/psum | solution.py:273
  (30 other events, 839.2 us)
Sparse Core Ops, SparseCore 0:
  136.1 92.0 all-gather.2
  491.4 88.7 all-gather.4
  584.1 87.2 all-reduce.1
